TPU v7x, 32 devices: a whole 2x2x4 slice. The times are simulated.
32 devices in a mesh: dp: 4 (over z), vocab: 8 (over y, x, core).
Axes of the slice: x: 2, y: 2, z: 4, core: 2. Of those that a mesh axis runs over, the one named last changes fastest.
Arguments:
- base_hidden: bfloat16 [96, 8192], P('dp', 'vocab'), may hold values from -16 to 16
- reinforced_hidden: bfloat16 [96, 8192], P('dp', 'vocab'), may hold values from -16 to 16
- trained_hidden: bfloat16 [96, 8192], P('dp', 'vocab'), may hold values from -16 to 16
- frozen_head: bfloat16 [8192, 16384], P(None, ('dp', 'vocab')), may hold values from -1 to 1
- trained_head: bfloat16 [8192, 16384], P(None, ('dp', 'vocab')), may hold values from -1 to 1
- label_tokens: int32 [96], P('dp'), may hold values from 0 to 16383
- generic_map: int32 [16384], replicated, may hold values from 0 to 16383, as said below
- loss_mask: int32 [96], P('dp'), may hold values 0 or 1
Outputs:
- token_loss: float32 [96], P('dp')
- head_grad: bfloat16 [8192, 16384], P(None, ('dp', 'vocab'))
- hidden_grad: bfloat16 [96, 8192], P('dp', 'vocab')
Inputs may be any that keep to these rules, and one draw needn't show every extreme that they name: `generic_map`: maps each token to its generic counterpart; many tokens map to themselves.
All inputs are finite; a program needn't handle non-finite values. No bound on the sum of `loss_mask` on one device may be relied on, other than what follows from the above.
Results may differ from a plain program's by a relative error of at most 0.0065.
Values may be sent and summed in bfloat16 or wider, within the bound.
No kernel may reach another device: no remote copies, remote signals or barrier semaphores. Data moves between devices by JAX's collectives and lax.ppermute only.
A program may use at most 128 MiB of HBM per device.

v0:
```python
import jax
import jax.numpy as jnp
from jax import lax
from jax.sharding import PartitionSpec as P

reinforce_weight = 2.0
anchor_share = 0.3
loss_scale = 16.0


def on_device(
    base_hidden,
    reinforced_hidden,
    trained_hidden,
    frozen_head,
    trained_head,
    label_tokens,
    generic_map,
    loss_mask,
):
    tok_local = base_hidden.shape[0]
    feature_local = base_hidden.shape[1]
    dp_count = lax.axis_size("dp")
    vocab_count = lax.axis_size("vocab")
    wide_rows = (
        lax.all_gather(base_hidden, "vocab", axis=1, tiled=True),
        lax.all_gather(reinforced_hidden, "vocab", axis=1, tiled=True),
        lax.all_gather(trained_hidden, "vocab", axis=1, tiled=True),
    )
    base_rows, reinforced_rows, trained_rows = (
        lax.all_gather(wide_rows[0], "dp", axis=0, tiled=True),
        lax.all_gather(wide_rows[1], "dp", axis=0, tiled=True),
        lax.all_gather(wide_rows[2], "dp", axis=0, tiled=True),
    )
    all_labels = (
        lax.all_gather(label_tokens, "dp", axis=0, tiled=True),
        lax.all_gather(loss_mask, "dp", axis=0, tiled=True),
    )
    labels_all, mask_all = all_labels
    base_logits = jnp.dot(base_rows, frozen_head, preferred_element_type=jnp.float32)
    reinforced_logits = jnp.dot(reinforced_rows, frozen_head, preferred_element_type=jnp.float32)
    generic = base_logits - reinforce_weight * jnp.maximum(reinforced_logits - base_logits, 0.0)
    trained_logits = jnp.dot(trained_rows, trained_head, preferred_element_type=jnp.float32)
    vocab_local = trained_head.shape[1]
    vocab_start = lax.axis_index(("dp", "vocab")) * vocab_local
    anchor = generic_map[labels_all]
    anchor_hit = (vocab_start + lax.iota(jnp.int32, vocab_local))[None, :] == anchor[:, None]
    picked_local = jnp.sum(jnp.where(anchor_hit, trained_logits, 0.0), axis=1)
    generic_peak, trained_peak = lax.pmax(
        (jnp.max(generic, axis=1), jnp.max(trained_logits, axis=1)), ("dp", "vocab")
    )
    generic_exps = jnp.exp(generic - generic_peak[:, None])
    trained_exps = jnp.exp(trained_logits - trained_peak[:, None])
    generic_total, cross_term, trained_total, picked_logit = lax.psum(
        (
            jnp.sum(generic_exps, axis=1),
            jnp.sum(generic_exps * trained_logits, axis=1),
            jnp.sum(trained_exps, axis=1),
            picked_local,
        ),
        ("dp", "vocab"),
    )
    token_weight = mask_all.astype(jnp.float32)
    loss_all = token_weight * (
        trained_peak
        + jnp.log(trained_total)
        - (1.0 - anchor_share) * cross_term / generic_total
        - anchor_share * picked_logit
    )
    token_loss = lax.dynamic_slice_in_dim(loss_all, lax.axis_index("dp") * tok_local, tok_local, 0)
    target = (1.0 - anchor_share) * generic_exps / generic_total[
        :, None
    ] + anchor_share * anchor_hit.astype(jnp.float32)
    logit_grad = (
        loss_scale * token_weight[:, None] * (trained_exps / trained_total[:, None] - target)
    ).astype(jnp.bfloat16)
    head_total = lax.dot_general(
        trained_rows, logit_grad, (((0,), (0,)), ((), ())), preferred_element_type=jnp.float32
    )
    grad_blocks = logit_grad.reshape(dp_count, tok_local, vocab_local)
    head_blocks = trained_head.reshape(vocab_count, feature_local, vocab_local)
    hidden_terms = jnp.einsum(
        "atv,bdv->abtd", grad_blocks, head_blocks, preferred_element_type=jnp.float32
    )
    hidden_terms = hidden_terms.reshape(dp_count * vocab_count * tok_local, feature_local)
    hidden_total = lax.psum_scatter(hidden_terms, ("dp", "vocab"), scatter_dimension=0, tiled=True)
    return (token_loss, head_total.astype(jnp.bfloat16), hidden_total.astype(jnp.bfloat16))


def solution(mesh):
    placed = (
        P("dp", "vocab"),
        P("dp", "vocab"),
        P("dp", "vocab"),
        P(None, ("dp", "vocab")),
        P(None, ("dp", "vocab")),
        P("dp"),
        P(),
        P("dp"),
    )
    return jax.shard_map(
        on_device,
        mesh=mesh,
        in_specs=placed,
        out_specs=(P("dp"), P(None, ("dp", "vocab")), P("dp", "vocab")),
        check_vma=False,
    )
```

profile of v0, /device:TPU:0, one launch (start us, length us, event | category | flops | bytes accessed | tf_op | source)
XLA Modules:
  0.0 336.3 jit_solution(8015253757386036704)
XLA Ops:
  7.2 12.9 %all_gather.27 = bf16[24,8192]{1,0:T(8,128)(2,1)} all-gather(bf16[24,1024]{1,0:T(8,128)(2,1)} %param.8), channel_id=1, replica_groups=mesh['dp'=4,'vocab'=8] {'vocab'}, dimensions={1}, use_global_device_ids=true | all-gather | bytes 442368 | tf_op jit(solution)/shard_map/all_gather | solution.py:26
  20.2 10.5 %all_gather.29 = bf16[24,8192]{1,0:T(8,128)(2,1)} all-gather(bf16[24,1024]{1,0:T(8,128)(2,1)} %param.9), channel_id=1, replica_groups=mesh['dp'=4,'vocab'=8] {'vocab'}, dimensions={1}, use_global_device_ids=true | all-gather | bytes 442368 | tf_op jit(solution)/shard_map/all_gather | solution.py:27
  30.7 10.5 %all_gather.25 = bf16[24,8192]{1,0:T(8,128)(2,1)} all-gather(bf16[24,1024]{1,0:T(8,128)(2,1)} %param.10), channel_id=1, replica_groups=mesh['dp'=4,'vocab'=8] {'vocab'}, dimensions={1}, use_global_device_ids=true | all-gather | bytes 442368 | tf_op jit(solution)/shard_map/all_gather | solution.py:28
  41.3 1.2 dynamic-slice
  43.2 0.9 dynamic-update-slice.1
  44.1 0.8 dynamic-update-slice
  44.9 9.1 %all-reduce.2 = (s32[96]{0:T(128)S(1)}, s32[96]{0:T(128)S(1)}) all-reduce(s32[96]{0:T(128)S(1)} %dynamic-update-slice.1, s32[96]{0:T(128)S(1)} %dynamic-update-slice), channel_id=1, replica_groups=mesh['dp'=4,'vocab'=8] {'dp'}, use_global_device_ids=true, to_apply=%add.1 | all-reduce | flops 192 | bytes 1536
  54.1 1.1 gather_fusion
  55.2 2.5 all-gather.6.cloned.1.call-done
  57.8 5.3 %fusion.13 = f32[96,512]{1,0:T(8,128)S(1)} fusion(bf16[96,8192]{1,0:T(8,128)(2,1)} %all-gather.6.cloned.1.call-done, bf16[8192,512]{1,0:T(8,128)(2,1)} %param.11), kind=kOutput, calls=%fused_computation.26 | convolution fusion | flops 805306368 | bytes 10158080 | tf_op jit(solution)/shard_map/dot_general | solution.py:40
  63.1 32.2 %all-gather.8.cloned.1.call-done = bf16[96,8192]{1,0:T(8,128)(2,1)} async-done(((bf16[24,8192]{1,0:T(8,128)(2,1)}), bf16[96,8192]{1,0:T(8,128)(2,1)}) %all-gather.8.cloned.1.call-update) | async-done | bytes 1572880 | tf_op jit(solution)/shard_map/all_gather | solution.py:32
  95.3 5.4 %fusion.12 = (f32[96]{0:T(128)S(1)}, f32[96,512]{1,0:T(8,128)S(1)}) fusion(f32[96,512]{1,0:T(8,128)S(1)} %fusion.13, bf16[96,8192]{1,0:T(8,128)(2,1)} %all-gather.8.cloned.1.call-done, bf16[8192,512]{1,0:T(8,128)(2,1)} %param.11), kind=kOutput, calls=%fused_computation.25 | convolution fusion | flops 805552000 | bytes 10355072 | tf_op jit(solution)/shard_map/dot_general | solution.py:41
  100.7 32.1 %all-gather.4.cloned.1.call-done = bf16[96,8192]{1,0:T(8,128)(2,1)} async-done(((bf16[24,8192]{1,0:T(8,128)(2,1)}), bf16[96,8192]{1,0:T(8,128)(2,1)}) %all-gather.4.cloned.1.call-update) | async-done | bytes 1572880 | tf_op jit(solution)/shard_map/all_gather | solution.py:33
  132.8 5.4 %fusion.11 = (f32[96]{0:T(128)S(1)}, f32[96,512]{1,0:T(8,128)S(1)}) fusion(bf16[96,8192]{1,0:T(8,128)(2,1)} %all-gather.4.cloned.1.call-done, bf16[8192,512]{1,0:T(8,128)(2,1)} %param.12), kind=kOutput, calls=%fused_computation.24 | convolution fusion | flops 805355392 | bytes 10158464 | tf_op jit(solution)/shard_map/dot_general | solution.py:43
  138.2 39.2 %all-reduce.4 = (f32[96]{0:T(128)S(1)}, f32[96]{0:T(128)S(1)}) all-reduce(f32[96]{0:T(128)S(1)} %get-tuple-element.25, f32[96]{0:T(128)S(1)} %get-tuple-element.27), channel_id=1, replica_groups=mesh['dp'=4,'vocab'=8] {'dp','vocab'}, use_global_device_ids=true, to_apply=%region_1.2 | all-reduce | flops 192 | bytes 1536 | tf_op jit(solution)/shard_map/pmax | solution.py:49
  177.4 0.3 fusion.9
  177.7 40.1 %all-reduce.3 = (f32[96]{0:T(128)S(1)}, f32[96]{0:T(128)S(1)}, f32[96]{0:T(128)S(1)}, f32[96]{0:T(128)S(1)}) all-reduce(f32[96]{0:T(128)S(1)} %get-tuple-element.12, f32[96]{0:T(128)S(1)} %get-tuple-element.13, f32[96]{0:T(128)S(1)} %get-tuple-element.14, f32[96]{0:T(128)S(1)} %get-tuple-element.11), channel_id=1, replica_groups=mesh['dp'=4,'vocab'=8] {'dp','vocab'}, use_global_device_ids=true, to_apply=%region_11.12 | all-reduce | flops 384 | bytes 3072 | tf_op jit(solution)/shard_map/psum | solution.py:54
  217.8 0.2 fusion.8
  218.0 7.9 %fusion.14 = f32[4,24,8,1024]{3,1,2,0:T(8,128)} fusion(bf16[4,24,512,1]{2,1,3,0:T(8,128)(2,1)S(1)} %bitcast.26, bf16[8,1024,512,1]{2,1,0,3:T(8,128)(2,1)} %bitcast.24), kind=kOutput, calls=%fused_computation.27 | convolution fusion | flops 805306368 | bytes 11632640 | tf_op jit(solution)/shard_map/atv,bdv->abtd/dot_general | solution.py:82
  226.0 5.6 %fusion = bf16[8192,512]{0,1:T(8,128)(2,1)} fusion(bf16[96,512]{1,0:T(8,128)(2,1)S(1)} %fusion.8, bf16[96,8192]{1,0:T(8,128)(2,1)S(1)} %copy-done.1), kind=kOutput, calls=%fused_computation.2 | convolution fusion | flops 809500672 | bytes 10059776 | tf_op jit(solution)/shard_map/dot_general | solution.py:77
  231.5 12.0 %copy.12 = bf16[8192,512]{1,0:T(8,128)(2,1)} copy(bf16[8192,512]{0,1:T(8,128)(2,1)} %fusion) | data formatting | bytes 16777216
  243.6 0.6 dynamic_slice.3
  244.2 84.1 %reduce-scatter.2.cloned.1.call-done = f32[24,1024]{1,0:T(8,128)} async-done(((f32[768,1024]{1,0:T(8,128)}), f32[24,1024]{1,0:T(8,128)}) %reduce-scatter.2.cloned.1.call-update) | async-done | bytes 98320 | tf_op jit(solution)/shard_map/reduce_scatter | solution.py:86
  328.2 1.5 convert_element_type.20
  (18 shorter events, 0.3 us)
Async XLA Ops:
  7.2 46.9 %copy-start = (s32[16384]{0:T(1024)S(1)}, s32[16384]{0:T(1024)}, u32[]{:S(2)}) copy-start(s32[16384]{0:T(1024)} %param.14) | copy-start | bytes 196612
  7.2 50.6 %all-gather.6.cloned.1.call-start = ((), (), s32[]{:S(2)}) async-start(), calls=%async_computation.2 | async-start | bytes 1966080 | tf_op jit(solution)/shard_map/all_gather | solution.py:31
  20.2 75.1 %all-gather.8.cloned.1.call-start = ((), (), s32[]{:S(2)}) async-start(), calls=%async_computation.3 | async-start | bytes 1966080 | tf_op jit(solution)/shard_map/all_gather | solution.py:32
  30.7 102.1 %all-gather.4.cloned.1.call-start = ((), (), s32[]{:S(2)}) async-start(), calls=%async_computation.1 | async-start | bytes 1966080 | tf_op jit(solution)/shard_map/all_gather | solution.py:33
  41.2 287.0 %reduce-scatter.2.cloned.1.call-start = ((), (), s32[]{:S(2)}) async-start(), calls=%async_computation.4 | async-start | bytes 3244032 | tf_op jit(solution)/shard_map/reduce_scatter | solution.py:86
  218.0 8.0 %copy-start.1 = (bf16[96,8192]{1,0:T(8,128)(2,1)S(1)}, bf16[96,8192]{1,0:T(8,128)(2,1)}, u32[]{:S(2)}) copy-start(bf16[96,8192]{1,0:T(8,128)(2,1)} %all-gather.4.cloned.1.call-done) | copy-start | bytes 4718596
Sparse Core Ops, SparseCore 0:
  20.3 37.4 all-gather.5
  59.3 35.8 all-gather.7
  96.8 35.8 all-gather.3
  226.1 102.1 reduce-scatter.1
where the time goes:
time: 337 us; the launch traced here: 336 us
  waiting for transfers between devices  151 us (45%)
  blocking collectives  122 us (36%)
  matrix products  29.7 us (9%)
  local copies, waits for them, and re-layouts  16.7 us (5%)
  between operations  14.5 us (4%)
    reduce_scatter x1, waiting for transfers between devices, on_device(): lax.psum_scatter(hidden_terms, ('dp', 'vocab'), scatter_dimension=0, tile...  84.1 us
    psum x1, blocking collectives, on_device(): lax.psum((jnp.sum(generic_exps, axis=1), jnp.sum(generic_exps * trained_l...  40.1 us
    pmax x1, blocking collectives, on_device(): lax.pmax((jnp.max(generic, axis=1), jnp.max(trained_logits, axis=1)), ('d...  39.2 us
    all_gather x1, waiting for transfers between devices, on_device(): lax.all_gather(wide_rows[1], 'dp', axis=0, tiled=True)  32.2 us
    all_gather x1, waiting for transfers between devices, on_device(): lax.all_gather(wide_rows[2], 'dp', axis=0, tiled=True)  32.1 us
    unnamed x10, local copies, waits for them, and re-layouts  15 us
    all_gather x1, blocking collectives, on_device(): lax.all_gather(base_hidden, 'vocab', axis=1, tiled=True)  12.9 us
    all_gather x1, blocking collectives, on_device(): lax.all_gather(trained_hidden, 'vocab', axis=1, tiled=True)  10.5 us
  transfers between devices with their start and end apart: 4, of which 4 were waited for; matrix products, arithmetic and copies ran while one was open for 10% of the time, Pallas kernels for 0%

commit v1 on v0

--- a/solution.py
+++ b/solution.py
@@ -6,6 +6,19 @@
 reinforce_weight = 2.0
 anchor_share = 0.3
 loss_scale = 16.0
+
+
+def gather_around(shard, axis, dim):
+    size, index, span = (lax.axis_size(axis), lax.axis_index(axis), shard.shape[dim])
+    ahead = [(i, (i + 1) % size) for i in range(size)]
+    filled = jnp.zeros((*shard.shape[:dim], size * span, *shard.shape[dim + 1 :]), shard.dtype)
+    held = shard
+    for step in range(size):
+        owner = (index - step) % size
+        filled = lax.dynamic_update_slice_in_dim(filled, held, owner * span, axis=dim)
+        if step < size - 1:
+            held = lax.ppermute(held, axis, ahead)
+    return filled
 
 
 def on_device(
@@ -29,7 +42,7 @@
     )
     base_rows, reinforced_rows, trained_rows = (
         lax.all_gather(wide_rows[0], "dp", axis=0, tiled=True),
-        lax.all_gather(wide_rows[1], "dp", axis=0, tiled=True),
+        gather_around(wide_rows[1], "dp", 0),
         lax.all_gather(wide_rows[2], "dp", axis=0, tiled=True),
     )
     all_labels = (

time: 337 us -> 318 us (0.944)
  waiting for transfers between devices: 151 us -> 120 us
  starting transfers between devices: 0.16 us -> 12.4 us
    all_gather x1 -> x0, waiting for transfers between devices: 32.2 us -> none  [on_device(): lax.all_gather(wide_rows[1], 'dp', axis=0, tiled=True)]
    ppermute x0 -> x3, waiting for transfers between devices: none -> 29.4 us  [gather_around(): held = lax.ppermute(held, axis, ahead)]
    all_gather x1, waiting for transfers between devices: 32.1 us -> 7.64 us  [on_device(): lax.all_gather(wide_rows[2], 'dp', axis=0, tiled=True)]
    ppermute x0 -> x3, starting transfers between devices: none -> 12.3 us  [gather_around(): held = lax.ppermute(held, axis, ahead)]
    unnamed x10 -> x16, local copies, waits for them, and re-layouts: 15 us -> 14.5 us
  transfers between devices with their start and end apart: 4 -> 6, of which waited for: 4 -> 4; matrix products, arithmetic and copies ran while one was open for 10% -> 10% of each run, Pallas kernels for 0% -> 0%
where the time goes in v1:
time: 318 us; the launch traced here: 317 us
  blocking collectives  122 us (38%)
  waiting for transfers between devices  120 us (38%)
  matrix products  29.1 us (9%)
  local copies, waits for them, and re-layouts  16.5 us (5%)
  between operations  14.7 us (5%)
  starting transfers between devices  12.4 us (4%)
    reduce_scatter x1, waiting for transfers between devices, on_device(): lax.psum_scatter(hidden_terms, ('dp', 'vocab'), scatter_dimension=0, tile...  82.8 us
    psum x1, blocking collectives, on_device(): lax.psum((jnp.sum(generic_exps, axis=1), jnp.sum(generic_exps * trained_l...  40.8 us
    pmax x1, blocking collectives, on_device(): lax.pmax((jnp.max(generic, axis=1), jnp.max(trained_logits, axis=1)), ('d...  38.5 us
    ppermute x3, waiting for transfers between devices, gather_around(): held = lax.ppermute(held, axis, ahead)  29.4 us
    unnamed x16, local copies, waits for them, and re-layouts  14.5 us
    all_gather x1, blocking collectives, on_device(): lax.all_gather(base_hidden, 'vocab', axis=1, tiled=True)  12.9 us
    ppermute x3, starting transfers between devices, gather_around(): held = lax.ppermute(held, axis, ahead)  12.3 us
    unnamed x1, blocking collectives  10.7 us
  transfers between devices with their start and end apart: 6, of which 4 were waited for; matrix products, arithmetic and copies ran while one was open for 10% of the time, Pallas kernels for 0%

profile of v1, /device:TPU:0, one launch (start us, length us, event | category | flops | bytes accessed | tf_op | source)
XLA Modules:
  0.0 316.8 jit_solution(1416778297748360266)
XLA Ops:
  7.3 12.9 %all_gather.24 = bf16[24,8192]{1,0:T(8,128)(2,1)} all-gather(bf16[24,1024]{1,0:T(8,128)(2,1)} %param.8), channel_id=1, replica_groups=mesh['dp'=4,'vocab'=8] {'vocab'}, dimensions={1}, use_global_device_ids=true | all-gather | bytes 442368 | tf_op jit(solution)/shard_map/all_gather | solution.py:39
  20.2 8.9 %all_gather.26 = bf16[24,8192]{1,0:T(8,128)(2,1)S(1)} all-gather(bf16[24,1024]{1,0:T(8,128)(2,1)} %param.9), channel_id=1, replica_groups=mesh['dp'=4,'vocab'=8] {'vocab'}, dimensions={1}, use_global_device_ids=true | all-gather | bytes 442368 | tf_op jit(solution)/shard_map/all_gather | solution.py:40
  29.1 1.6 collective-permute-start
  30.7 10.4 %all_gather.22 = bf16[24,8192]{1,0:T(8,128)(2,1)} all-gather(bf16[24,1024]{1,0:T(8,128)(2,1)} %param.10), channel_id=1, replica_groups=mesh['dp'=4,'vocab'=8] {'vocab'}, dimensions={1}, use_global_device_ids=true | all-gather | bytes 442368 | tf_op jit(solution)/shard_map/all_gather | solution.py:41
  41.3 0.6 dynamic-slice
  43.0 10.7 %all-reduce.2 = (s32[96]{0:T(128)S(1)}, s32[96]{0:T(128)S(1)}) all-reduce(s32[96]{0:T(128)S(1)} %dynamic-update-slice.1, s32[96]{0:T(128)S(1)} %dynamic-update-slice), channel_id=1, replica_groups=mesh['dp'=4,'vocab'=8] {'dp'}, use_global_device_ids=true, to_apply=%add.1 | all-reduce | flops 192 | bytes 1536
  53.9 1.1 gather_fusion
  55.1 10.3 %collective-permute-start.1 = (bf16[24,8192]{1,0:T(8,128)(2,1)S(1)}, bf16[24,8192]{1,0:T(8,128)(2,1)S(1)}, u32[]{:S(2)}, u32[]{:S(2)}) collective-permute-start(bf16[24,8192]{1,0:T(8,128)(2,1)S(1)} %collective-permute-done), channel_id=1, source_target_pairs={{0,8},{8,16},{16,24},{24,0},{1,9},{9,17},{17,25},{25,1},{2,10},{10... | collective-permute-start | bytes 1179656 | tf_op jit(solution)/shard_map/ppermute | solution.py:20
  65.4 9.6 %collective-permute-done.1 = bf16[24,8192]{1,0:T(8,128)(2,1)S(1)} collective-permute-done((bf16[24,8192]{1,0:T(8,128)(2,1)S(1)}, bf16[24,8192]{1,0:T(8,128)(2,1)S(1)}, u32[]{:S(2)}, u32[]{:S(2)}) %collective-permute-start.1) | collective-permute-done | bytes 393248 | tf_op jit(solution)/shard_map/ppermute | solution.py:20
  75.0 0.4 collective-permute-start.2
  75.5 19.8 %collective-permute-done.2 = bf16[24,8192]{1,0:T(8,128)(2,1)S(1)} collective-permute-done((bf16[24,8192]{1,0:T(8,128)(2,1)S(1)}, bf16[24,8192]{1,0:T(8,128)(2,1)S(1)}, u32[]{:S(2)}, u32[]{:S(2)}) %collective-permute-start.2) | collective-permute-done | bytes 393248 | tf_op jit(solution)/shard_map/ppermute | solution.py:20
  95.3 5.4 %fusion.13 = f32[96,512]{1,0:T(8,128)S(1)} fusion(bf16[96,8192]{1,0:T(8,128)(2,1)} %all-gather.5.cloned.1.call-done, bf16[8192,512]{1,0:T(8,128)(2,1)} %param.11), kind=kOutput, calls=%fused_computation.30 | convolution fusion | flops 805306368 | bytes 10158080 | tf_op jit(solution)/shard_map/dot_general | solution.py:53
  100.7 5.0 %fusion.12 = (f32[96]{0:T(128)S(1)}, f32[96,512]{1,0:T(8,128)S(1)}) fusion(f32[96,512]{1,0:T(8,128)S(1)} %fusion.13, bf16[96,8192]{1,0:T(8,128)(2,1)S(1)} %constant_dynamic-update-slice_fusion, bf16[8192,512]{1,0:T(8,128)(2,1)} %param.11), kind=kOutput, calls=%fused_computation.29 | convolution fusion | flops 805552000 | bytes 10355072 | tf_op jit(solution)/shard_map/dot_general | solution.py:54
  105.7 7.6 %all-gather.3.cloned.1.call-done = bf16[96,8192]{1,0:T(8,128)(2,1)} async-done(((bf16[24,8192]{1,0:T(8,128)(2,1)}), bf16[96,8192]{1,0:T(8,128)(2,1)}) %all-gather.3.cloned.1.call-update) | async-done | bytes 1572880 | tf_op jit(solution)/shard_map/all_gather | solution.py:46
  113.3 5.4 %fusion.11 = (f32[96]{0:T(128)S(1)}, f32[96,512]{1,0:T(8,128)S(1)}) fusion(bf16[96,8192]{1,0:T(8,128)(2,1)} %all-gather.3.cloned.1.call-done, bf16[8192,512]{1,0:T(8,128)(2,1)} %param.12), kind=kOutput, calls=%fused_computation.28 | convolution fusion | flops 805355392 | bytes 10158464 | tf_op jit(solution)/shard_map/dot_general | solution.py:56
  118.8 38.5 %all-reduce.4 = (f32[96]{0:T(128)S(1)}, f32[96]{0:T(128)S(1)}) all-reduce(f32[96]{0:T(128)S(1)} %get-tuple-element.25, f32[96]{0:T(128)S(1)} %get-tuple-element.27), channel_id=1, replica_groups=mesh['dp'=4,'vocab'=8] {'dp','vocab'}, use_global_device_ids=true, to_apply=%region_1.2 | all-reduce | flops 192 | bytes 1536 | tf_op jit(solution)/shard_map/pmax | solution.py:62
  157.5 40.8 %all-reduce.3 = (f32[96]{0:T(128)S(1)}, f32[96]{0:T(128)S(1)}, f32[96]{0:T(128)S(1)}, f32[96]{0:T(128)S(1)}) all-reduce(f32[96]{0:T(128)S(1)} %get-tuple-element.12, f32[96]{0:T(128)S(1)} %get-tuple-element.13, f32[96]{0:T(128)S(1)} %get-tuple-element.14, f32[96]{0:T(128)S(1)} %get-tuple-element.11), channel_id=1, replica_groups=mesh['dp'=4,'vocab'=8] {'dp','vocab'}, use_global_device_ids=true, to_apply=%region_11.12 | all-reduce | flops 384 | bytes 3072 | tf_op jit(solution)/shard_map/psum | solution.py:67
  198.6 7.8 %fusion.14 = f32[4,24,8,1024]{3,1,2,0:T(8,128)} fusion(bf16[4,24,512,1]{2,1,3,0:T(8,128)(2,1)S(1)} %bitcast.26, bf16[8,1024,512,1]{2,1,0,3:T(8,128)(2,1)} %bitcast.24), kind=kOutput, calls=%fused_computation.31 | convolution fusion | flops 805306368 | bytes 11632640 | tf_op jit(solution)/shard_map/atv,bdv->abtd/dot_general | solution.py:95
  206.4 1.4 copy-done.1
  207.8 5.6 %fusion = bf16[8192,512]{0,1:T(8,128)(2,1)} fusion(bf16[96,512]{1,0:T(8,128)(2,1)S(1)} %fusion.8, bf16[96,8192]{1,0:T(8,128)(2,1)S(1)} %copy-done.1), kind=kOutput, calls=%fused_computation.2 | convolution fusion | flops 809500672 | bytes 10059776 | tf_op jit(solution)/shard_map/dot_general | solution.py:90
  213.4 12.0 %copy.12 = bf16[8192,512]{1,0:T(8,128)(2,1)} copy(bf16[8192,512]{0,1:T(8,128)(2,1)} %fusion) | data formatting | bytes 16777216
  225.4 0.6 dynamic_slice.3
  226.0 82.8 %reduce-scatter.2.cloned.1.call-done = f32[24,1024]{1,0:T(8,128)} async-done(((f32[768,1024]{1,0:T(8,128)}), f32[24,1024]{1,0:T(8,128)}) %reduce-scatter.2.cloned.1.call-update) | async-done | bytes 98320 | tf_op jit(solution)/shard_map/reduce_scatter | solution.py:99
  308.7 1.5 convert_element_type.20
  (32 shorter events, 1.4 us)
Async XLA Ops:
  7.2 46.8 %copy-start = (s32[16384]{0:T(1024)S(1)}, s32[16384]{0:T(1024)}, u32[]{:S(2)}) copy-start(s32[16384]{0:T(1024)} %param.14) | copy-start | bytes 196612
  7.2 34.1 %copy-start.4 = (u32[32]{0:T(128)S(1)}, u32[32]{0:T(128)}, u32[]{:S(2)}) copy-start(u32[32]{0:T(128)} %constant.74) | copy-start | bytes 388
  7.2 35.3 %copy-start.2 = (s32[24]{0:T(128)S(1)}, s32[24]{0:T(128)}, u32[]{:S(2)}) copy-start(s32[24]{0:T(128)} %param.13) | copy-start | bytes 292
  7.2 35.6 %copy-start.3 = (s32[24]{0:T(128)S(1)}, s32[24]{0:T(128)}, u32[]{:S(2)}) copy-start(s32[24]{0:T(128)} %param.15) | copy-start | bytes 292
  7.2 88.1 %all-gather.5.cloned.1.call-start = ((), (), s32[]{:S(2)}) async-start(), calls=%async_computation.2 | async-start | bytes 1966080 | tf_op jit(solution)/shard_map/all_gather | solution.py:44
  20.2 93.1 %all-gather.3.cloned.1.call-start = ((), (), s32[]{:S(2)}) async-start(), calls=%async_computation.1 | async-start | bytes 1966080 | tf_op jit(solution)/shard_map/all_gather | solution.py:46
  29.1 26.0 %collective-permute-start = (bf16[24,8192]{1,0:T(8,128)(2,1)S(1)}, bf16[24,8192]{1,0:T(8,128)(2,1)S(1)}, u32[]{:S(2)}, u32[]{:S(2)}) collective-permute-start(bf16[24,8192]{1,0:T(8,128)(2,1)S(1)} %all_gather.26), channel_id=1, source_target_pairs={{0,8},{8,16},{16,24},{24,0},{1,9},{9,17},{17,25},{25,1},{2,10},{10... | collective-permute-start | bytes 1179656 | tf_op jit(solution)/shard_map/ppermute | solution.py:20
  41.1 267.6 %reduce-scatter.2.cloned.1.call-start = ((), (), s32[]{:S(2)}) async-start(), calls=%async_computation.3 | async-start | bytes 3244032 | tf_op jit(solution)/shard_map/reduce_scatter | solution.py:99
  55.1 19.9 %collective-permute-start.1 = (bf16[24,8192]{1,0:T(8,128)(2,1)S(1)}, bf16[24,8192]{1,0:T(8,128)(2,1)S(1)}, u32[]{:S(2)}, u32[]{:S(2)}) collective-permute-start(bf16[24,8192]{1,0:T(8,128)(2,1)S(1)} %collective-permute-done), channel_id=1, source_target_pairs={{0,8},{8,16},{16,24},{24,0},{1,9},{9,17},{17,25},{25,1},{2,10},{10... | collective-permute-start | bytes 1179656 | tf_op jit(solution)/shard_map/ppermute | solution.py:20
  75.0 20.2 %collective-permute-start.2 = (bf16[24,8192]{1,0:T(8,128)(2,1)S(1)}, bf16[24,8192]{1,0:T(8,128)(2,1)S(1)}, u32[]{:S(2)}, u32[]{:S(2)}) collective-permute-start(bf16[24,8192]{1,0:T(8,128)(2,1)S(1)} %collective-permute-done.1), channel_id=1, source_target_pairs={{0,8},{8,16},{16,24},{24,0},{1,9},{9,17},{17,25},{25,1},{2,10},{10... | collective-permute-start | bytes 1179656 | tf_op jit(solution)/shard_map/ppermute | solution.py:20
  206.4 1.4 copy-start.1
Sparse Core Ops, SparseCore 0:
  20.3 46.6 all-gather.4
  68.5 44.7 all-gather.2
  206.5 102.1 reduce-scatter.1
